TPU v7x, 32 devices: a whole 2x2x4 slice. The times are simulated.
32 devices in a mesh: group: 2 (over core), dp: 4 (over z), section: 2 (over x), tensor: 2 (over y).
Axes of the slice: x: 2, y: 2, z: 4, core: 2. Of those that a mesh axis runs over, the one named last changes fastest.
Arguments:
- merged: bfloat16 [768, 5120], P('dp'), may hold values from -6 to 6
- counts: int32 [8], P('dp'), may hold values from 4 to 384
- owners: int32 [768, 1], P('dp'), may hold values from 0 to 3; in each aligned block of 192 rows (0 to 191, 192 to 383, ...) at most 96 rows name the same one
- w_merge: bfloat16 [5120, 8192], P(None, ('group', 'section', 'tensor')), may hold values from -0.078125 to 0.078125
- norm_gain: float32 [8192], P(('group', 'section', 'tensor')), may hold values from 0.25 to 1.75
- cotangent: bfloat16 [4, 4, 96, 8192], P('dp', None, None, ('group', 'section', 'tensor')), may hold values from -6 to 6
Outputs:
- embedded: bfloat16 [4, 4, 96, 8192], P('dp', None, None, ('group', 'section', 'tensor'))
- grad_merged: float32 [768, 5120], P('dp', ('group', 'section', 'tensor'))
- grad_weight: float32 [5120, 8192], P('dp', ('group', 'section', 'tensor'))
Inputs may be any that keep to these rules, and one draw needn't show every extreme that they name: `owners`: in each replica's 192 rows no owner appears more than 96 times.
All inputs are finite; a program needn't handle non-finite values.
Results may differ from a plain program's by a relative error of at most 0.0049.
Values may be sent and summed in bfloat16 or wider, within the bound.
A program may use at most 64 MiB of HBM per device.

v0:
```python
import jax
import jax.numpy as jnp
from jax import lax
from jax.sharding import PartitionSpec as P

D = 8192


def on_device(merged, counts, owners, w_merge, norm_gain, cotangent):
    rows = merged.shape[0]
    columns = w_merge.shape[1]
    replicas = lax.axis_size("dp")
    slots = cotangent.shape[2]
    images = counts.shape[0]
    per_image = rows // images
    projected = jnp.dot(merged, w_merge, preferred_element_type=jnp.float32).astype(jnp.bfloat16)
    row_index = jnp.arange(rows, dtype=jnp.int32)
    image_of = row_index // per_image
    picked = image_of[:, None] == jnp.arange(images, dtype=jnp.int32)[None, :]
    count_of = jnp.sum(jnp.where(picked, counts[None, :], 0), axis=1)
    valid = (4 * (row_index % per_image) < count_of).astype(jnp.float32)
    masked = (projected.astype(jnp.float32) * valid[:, None]).astype(jnp.bfloat16)
    owner = owners[:, 0]
    hits = (owner[:, None] == jnp.arange(replicas, dtype=jnp.int32)[None, :]).astype(jnp.int32)
    before = jnp.cumsum(hits, axis=0) - hits
    slot_index = jnp.sum(before * hits, axis=1)
    target = owner * slots + slot_index
    placer = (jnp.arange(replicas * slots, dtype=jnp.int32)[:, None] == target[None, :]).astype(
        jnp.bfloat16
    )
    outgoing = jnp.dot(placer, masked, preferred_element_type=jnp.float32).astype(jnp.bfloat16)
    outgoing = outgoing.reshape(replicas, slots, columns)
    received = lax.all_to_all(outgoing, "dp", split_axis=0, concat_axis=0, tiled=True)
    values = received.astype(jnp.float32)
    square_sums = lax.psum(jnp.sum(values * values, axis=2), ("group", "section", "tensor"))
    scale = lax.rsqrt(square_sums / D + 1e-05)
    normed = (values * scale[:, :, None] * norm_gain[None, None, :]).astype(jnp.bfloat16)
    embedded = normed[None]
    grad_in = cotangent[0].astype(jnp.float32) * norm_gain[None, None, :]
    inner_sums = lax.psum(jnp.sum(grad_in * values, axis=2), ("group", "section", "tensor"))
    inner = inner_sums / D
    slot_grad = (scale[:, :, None] * grad_in - values * (scale**3 * inner)[:, :, None]).astype(
        jnp.bfloat16
    )
    returned = lax.all_to_all(slot_grad, "dp", split_axis=0, concat_axis=0, tiled=True)
    returned = returned.reshape(replicas * slots, columns)
    gathered = lax.dot_general(
        placer, returned, (((0,), (0,)), ((), ())), preferred_element_type=jnp.float32
    )
    back = (gathered * valid[:, None]).astype(jnp.bfloat16)
    input_terms = lax.dot_general(
        back, w_merge, (((1,), (1,)), ((), ())), preferred_element_type=jnp.float32
    )
    grad_merged = lax.psum_scatter(
        input_terms, ("group", "section", "tensor"), scatter_dimension=1, tiled=True
    )
    column_block = lax.all_to_all(merged, "dp", split_axis=1, concat_axis=0, tiled=True)
    grad_weight = lax.dot_general(
        column_block,
        lax.all_gather(back, "dp", axis=0, tiled=True),
        (((0,), (0,)), ((), ())),
        preferred_element_type=jnp.float32,
    )
    return (embedded, grad_merged, grad_weight)


def solution(mesh):
    placed = (
        P("dp", None),
        P("dp"),
        P("dp", None),
        P(None, ("group", "section", "tensor")),
        P(("group", "section", "tensor")),
        P("dp", None, None, ("group", "section", "tensor")),
    )
    return jax.shard_map(
        on_device,
        mesh=mesh,
        in_specs=placed,
        out_specs=(
            P("dp", None, None, ("group", "section", "tensor")),
            P("dp", ("group", "section", "tensor")),
            P("dp", ("group", "section", "tensor")),
        ),
        check_vma=False,
    )
```

profile of v0, /device:TPU:0, one launch (start us, length us, event | category | flops | bytes accessed | tf_op | source)
XLA Modules:
  0.0 182.4 jit_solution(6930971145670902794)
XLA Ops:
  8.0 0.0 all-gather.2.cloned.1.call-start
  8.1 0.7 iota_compare_fusion.3
  8.7 0.7 fusion.18
  9.5 1.2 reduce-window.6
  10.8 0.1 slice.12
  10.8 0.1 copy.23
  11.0 0.1 copy.24
  11.1 0.1 add_bitcast_fusion
  11.2 0.7 fusion.16
  11.9 0.7 multiply_add_fusion
  12.5 0.0 copy-start.2
  12.5 7.0 %convolution_convert_fusion = bf16[384,1024]{1,0:T(8,128)(2,1)S(1)} fusion(bf16[192,5120]{1,0:T(8,128)(2,1)} %param.6, bf16[5120,1024]{1,0:T(8,128)(2,1)} %param.9, f32[192]{0:T(256)S(1)} %compare_convert_fusion, s32[192]{0:T(256)S(1)} %multiply_add_fusion), kind=kOutput, calls=%fused_computation.14 | convolution fusion | flops 2165514240 | bytes 13239808 | tf_op jit(solution)/shard_map/dot_general | solution.py:31
  19.6 0.0 copy-start
  19.6 26.4 %all_to_all.29 = bf16[4,96,1024]{2,1,0:T(8,128)(2,1)S(1)} all-to-all(bf16[4,96,1024]{2,1,0:T(8,128)(2,1)S(1)} %bitcast.38), channel_id=1, replica_groups=mesh['group'=2,'dp'=4,'section'=2,'tensor'=2] {'dp'}, dimensions={0} | all-to-all | bytes 1572864 | tf_op jit(solution)/shard_map/all_to_all | solution.py:33
  46.0 0.0 copy-done.2
  46.0 0.0 copy-done
  46.0 0.4 fusion.3
  46.4 14.3 %all-reduce.1 = (f32[4,96]{1,0:T(4,128)S(1)}, f32[4,96]{1,0:T(4,128)S(1)}) all-reduce(f32[4,96]{1,0:T(4,128)S(1)} %get-tuple-element.19, f32[4,96]{1,0:T(4,128)S(1)} %get-tuple-element.18), channel_id=1, replica_groups=mesh['group'=2,'dp'=4,'section'=2,'tensor'=2] {'group','section','tensor'}, use_global_device_ids=true, to_apply=%region_5.6 | all-reduce | flops 768 | bytes 6144 | tf_op jit(solution)/shard_map/psum | solution.py:35
  60.7 1.4 fusion.5
  62.1 23.6 %all_to_all.30 = bf16[4,96,1024]{2,1,0:T(8,128)(2,1)S(1)} all-to-all(bf16[4,96,1024]{2,1,0:T(8,128)(2,1)S(1)} %get-tuple-element.22), channel_id=1, replica_groups=mesh['group'=2,'dp'=4,'section'=2,'tensor'=2] {'dp'}, dimensions={0} | all-to-all | bytes 1572864 | tf_op jit(solution)/shard_map/all_to_all | solution.py:45
  85.7 1.2 fusion.7
  86.9 0.0 all-gather.2.cloned.1.call-update
  86.9 0.0 reduce-scatter.2.cloned.1.call-start
  86.9 9.7 %fusion.21 = f32[192,5120]{1,0:T(8,128)} fusion(bf16[192,1024]{1,0:T(8,128)(2,1)} %fusion.7, bf16[5120,1024]{1,0:T(8,128)(2,1)} %param.9), kind=kOutput, calls=%fused_computation.48 | convolution fusion | flops 2013265920 | bytes 14811136 | tf_op jit(solution)/shard_map/dot_general | solution.py:51
  96.7 0.0 copy-start.1
  96.7 0.0 reduce-scatter.2.cloned.1.call-update
  96.7 1.5 copy-done.1
  98.2 0.1 copy.31
  98.3 64.7 %all_to_all.31 = bf16[192,4,1280]{2,0,1:T(8,128)(2,1)S(1)} all-to-all(bf16[192,4,1280]{2,0,1:T(8,128)(2,1)S(1)} %bitcast.34), channel_id=1, replica_groups=mesh['group'=2,'dp'=4,'section'=2,'tensor'=2] {'dp'}, dimensions={1} | all-to-all | bytes 3932160 | tf_op jit(solution)/shard_map/all_to_all | solution.py:57
  163.1 0.0 all-gather.2.cloned.1.call-done
  163.1 6.0 %convolution_bitcast_fusion = f32[1280,1024]{0,1:T(8,128)} fusion(bf16[768,1024]{1,0:T(8,128)(2,1)} %all-gather.2.cloned.1.call-done, bf16[768,1280]{1,0:T(8,128)(2,1)S(1)} %bitcast.37), kind=kOutput, calls=%fused_computation | convolution fusion | flops 2013265920 | bytes 8781824 | tf_op jit(solution)/shard_map/dot_general | solution.py:58
  169.1 5.9 %copy.26 = f32[1280,1024]{1,0:T(8,128)} copy(f32[1280,1024]{0,1:T(8,128)} %convolution_bitcast_fusion) | data formatting | bytes 10485760
  174.9 0.0 reduce-scatter.2.cloned.1.call-done
  (8 shorter events, 0.1 us)
Async XLA Ops:
  8.0 155.1 %all-gather.2.cloned.1.call-start = ((), (), s32[]{:S(2)}) async-start(), calls=%async_computation.5 | async-start | bytes 1966080 | tf_op jit(solution)/shard_map/all_gather | solution.py:60
  12.5 33.4 %copy-start.2 = (f32[1024]{0:T(1024)S(1)}, f32[1024]{0:T(1024)}, u32[]{:S(2)}) copy-start(f32[1024]{0:T(1024)} %param.10) | copy-start | bytes 12292
  19.6 26.4 %copy-start = (bf16[1,4,96,1024]{3,2,1,0:T(8,128)(2,1)S(1)}, bf16[1,4,96,1024]{3,2,1,0:T(8,128)(2,1)}, u32[]{:S(2)}) copy-start(bf16[1,4,96,1024]{3,2,1,0:T(8,128)(2,1)} %param.11) | copy-start | bytes 2359300
  86.9 88.1 %reduce-scatter.2.cloned.1.call-start = ((), (), s32[]{:S(2)}) async-start(), calls=%async_computation.4 | async-start | bytes 4423680 | tf_op jit(solution)/shard_map/reduce_scatter | solution.py:54
  96.7 1.5 copy-start.1
Sparse Core Ops, SparseCore 0:
  87.0 58.4 all-gather.1
Sparse Core Ops, SparseCore 1:
  96.8 46.7 reduce-scatter.1
where the time goes:
time: 183 us; the launch traced here: 182 us
  blocking collectives  129 us (70%)
  matrix products  23.9 us (13%)
  between operations  15.5 us (8%)
  local copies, waits for them, and re-layouts  7.84 us (4%)
  other arithmetic  6.04 us (3%)
    all_to_all x1, blocking collectives, on_device(): lax.all_to_all(merged, 'dp', split_axis=1, concat_axis=0, tiled=True)  64.7 us
    all_to_all x1, blocking collectives, on_device(): lax.all_to_all(outgoing, 'dp', split_axis=0, concat_axis=0, tiled=True)  26.4 us
    all_to_all x1, blocking collectives, on_device(): lax.all_to_all(slot_grad, 'dp', split_axis=0, concat_axis=0, tiled=True)  23.6 us
    psum x1, blocking collectives, on_device(): lax.psum(jnp.sum(values * values, axis=2), ('group', 'section', 'tensor'))  14.3 us
    dot_general x1, matrix products, on_device(): lax.dot_general(back, w_merge, (((1,), (1,)), ((), ())), preferred_elemen...  9.72 us
    unnamed x8, local copies, waits for them, and re-layouts  7.42 us
    dot_general x1, matrix products, on_device(): jnp.dot(placer, masked, preferred_element_type=jnp.float32)  7.02 us
    dot_general x1, matrix products, on_device(): lax.dot_general(column_block, lax.all_gather(back, 'dp', axis=0, tiled=Tr...  5.97 us
  transfers between devices with their start and end apart: 2, of which 0 were waited for; matrix products, arithmetic and copies ran while one was open for 12% of the time, Pallas kernels for 0%

commit v1 on v0

--- a/solution.py
+++ b/solution.py
@@ -1,9 +1,18 @@
+import functools
+
 import jax
 import jax.numpy as jnp
 from jax import lax
+from jax.experimental import pallas as pl
+from jax.experimental.pallas import tpu as pltpu
 from jax.sharding import PartitionSpec as P
 
 D = 8192
+MESH = pl.DeviceIdType.MESH
+F32 = jnp.float32
+BF16 = jnp.bfloat16
+WCHUNKS = 5
+BCHUNKS = 4
 
 
 def on_device(merged, counts, owners, w_merge, norm_gain, cotangent):
@@ -64,7 +73,477 @@
     return (embedded, grad_merged, grad_weight)
 
 
+def remote(src, dst, send_sem, recv_sem, device):
+    return pltpu.make_async_remote_copy(
+        src_ref=src,
+        dst_ref=dst,
+        send_sem=send_sem,
+        recv_sem=recv_sem,
+        device_id=device,
+        device_id_type=MESH,
+    )
+
+
+def main_kernel(
+    sizes,
+    own_col,
+    own_row,
+    counts,
+    merged,
+    w_hbm,
+    gain_ref,
+    cot,
+    emb,
+    gm,
+    mblk,
+    back_all,
+    w,
+    cot_in,
+    outgoing,
+    masked,
+    stat_out,
+    stat_in,
+    pair_out,
+    pair_in,
+    plane_out,
+    plane_in,
+    w_sem,
+    zm_s,
+    zm_r,
+    zc_s,
+    zc_r,
+    ze_s,
+    ze_r,
+    st_s,
+    st_r,
+    pm_s,
+    pm_r,
+    gm_s,
+    gm_r,
+    bk_s,
+    bk_r,
+    po_s,
+    po_r,
+    pl_s,
+    pl_r,
+):
+    n, groups, sections, tensors = sizes
+    plane = sections * tensors
+    shards = groups * plane
+    rows, deep = merged.shape
+    cols = w.shape[1]
+    slots = cot.shape[1]
+    dblock = deep // n
+    half = dblock // groups
+    part = rows // plane
+    gcols = deep // shards
+    images = counts.shape[0]
+    per_image = rows // images
+    me = lax.axis_index("dp")
+    g = lax.axis_index("group")
+    st = lax.axis_index("section") * tensors + lax.axis_index("tensor")
+    f = g * plane + st
+
+    def dp_of(r):
+        return lax.rem(me + r, n)
+
+    def at_plane(gg, ss):
+        return {"group": gg, "section": ss // tensors, "tensor": lax.rem(ss, tensors)}
+
+    barrier = pltpu.get_barrier_semaphore()
+    for r in range(1, n):
+        pl.semaphore_signal(barrier, inc=1, device_id={"dp": dp_of(r)}, device_id_type=MESH)
+    for q in range(1, shards):
+        other = lax.rem(f + q, shards)
+        pl.semaphore_signal(
+            barrier,
+            inc=1,
+            device_id=at_plane(other // plane, lax.rem(other, plane)),
+            device_id_type=MESH,
+        )
+    wrows = deep // WCHUNKS
+    wcopies = []
+    for c in range(WCHUNKS):
+        copy = pltpu.make_async_copy(
+            w_hbm.at[pl.ds(c * wrows, wrows), :], w.at[pl.ds(c * wrows, wrows), :], w_sem.at[c]
+        )
+        copy.start()
+        wcopies.append(copy)
+    pl.semaphore_wait(barrier, n - 1 + shards - 1)
+
+    my_rows = pl.ds(pl.multiple_of(st * part, part), part)
+    my_cols = pl.ds(pl.multiple_of(g * half, half), half)
+    zm = []
+    zc = []
+    for r in range(1, n):
+        to = dp_of(r)
+        copy = remote(
+            merged.at[my_rows, pl.ds(pl.multiple_of(to * dblock + g * half, half), half)],
+            mblk.at[me, my_rows, my_cols],
+            zm_s.at[r - 1],
+            zm_r.at[r - 1],
+            {"dp": to},
+        )
+        copy.start()
+        zm.append(copy)
+    for r in range(1, n):
+        to = dp_of(r)
+        copy = remote(cot.at[to], cot_in.at[n - r], zc_s.at[r - 1], zc_r.at[n - r - 1], {"dp": to})
+        copy.start()
+        zc.append(copy)
+
+    acc = jnp.zeros((rows, cols), F32)
+    for c in range(WCHUNKS):
+        wcopies[c].wait()
+        acc = acc + jnp.dot(
+            merged[:, c * wrows : (c + 1) * wrows],
+            w[c * wrows : (c + 1) * wrows, :],
+            preferred_element_type=F32,
+        )
+
+    row_of = lax.broadcasted_iota(jnp.int32, (rows, 1), 0)
+    valid = jnp.zeros((rows, 1), F32)
+    for im in range(images):
+        inside = (row_of >= im * per_image) & (row_of < (im + 1) * per_image)
+        seen = inside & (4 * (row_of - im * per_image) < counts[im])
+        valid = jnp.where(seen, 1.0, valid)
+    masked[...] = acc.astype(BF16).astype(F32) * valid
+    values = masked[...]
+
+    wide = stat_out.shape[2]
+    eye = lax.broadcasted_iota(jnp.int32, (rows, wide), 0) == lax.broadcasted_iota(
+        jnp.int32, (rows, wide), 1
+    )
+
+    def send_stat(which, column):
+        line = jnp.sum(jnp.where(eye, column, 0.0), axis=0, keepdims=True)
+        line = jnp.broadcast_to(line, (8, wide))
+        stat_out[which] = line
+        stat_in[which, f] = line
+        copies = []
+        for q in range(1, shards):
+            other = lax.rem(f + q, shards)
+            copy = remote(
+                stat_out.at[which],
+                stat_in.at[which, f],
+                st_s.at[which, q - 1],
+                st_r.at[which, q - 1],
+                at_plane(other // plane, lax.rem(other, plane)),
+            )
+            copy.start()
+            copies.append(copy)
+        return copies
+
+    def take_stat(which, copies):
+        for copy in copies:
+            copy.wait()
+        line = stat_in[which, 0]
+        for other in range(1, shards):
+            line = line + stat_in[which, other]
+        return jnp.sum(jnp.where(eye, line[0:1], 0.0), axis=1, keepdims=True)
+
+    squares = send_stat(0, jnp.sum(values * values, axis=1, keepdims=True))
+
+    oc = own_col[...]
+    orow = own_row[...]
+    hits_c = (oc == lax.broadcasted_iota(jnp.int32, (rows, n), 1)).astype(F32)
+    hits_r = (orow == lax.broadcasted_iota(jnp.int32, (n, rows), 0)).astype(F32)
+    i0 = lax.broadcasted_iota(jnp.int32, (rows, rows), 0)
+    i1 = lax.broadcasted_iota(jnp.int32, (rows, rows), 1)
+    lower = (i1 < i0).astype(F32).astype(BF16)
+    upper = (i0 < i1).astype(F32).astype(BF16)
+    before_c = jnp.dot(lower, hits_c.astype(BF16), preferred_element_type=F32)
+    before_r = jnp.dot(hits_r.astype(BF16), upper, preferred_element_type=F32)
+    slot_c = jnp.sum(before_c * hits_c, axis=1, keepdims=True).astype(jnp.int32)
+    slot_r = jnp.sum(before_r * hits_r, axis=0, keepdims=True).astype(jnp.int32)
+    rel_c = jnp.where(oc < me, oc - me + n, oc - me)
+    rel_r = jnp.where(orow < me, orow - me + n, orow - me)
+    tgt_c = rel_c * slots + slot_c
+    tgt_r = rel_r * slots + slot_r
+    gain = gain_ref[...]
+
+    mblk[me] = merged[:, pl.ds(pl.multiple_of(me * dblock, dblock), dblock)]
+
+    scale = lax.rsqrt(take_stat(0, squares) / D + 1e-05)
+    normed = (values * scale * gain).astype(BF16)
+    ze = []
+    for r in range(n):
+        place = (
+            lax.broadcasted_iota(jnp.int32, (slots, rows), 0) + r * slots == tgt_r
+        ).astype(F32).astype(BF16)
+        block = jnp.dot(place, normed, preferred_element_type=F32).astype(BF16)
+        if r == 0:
+            emb[me] = block
+        else:
+            outgoing[r - 1] = block
+            copy = remote(
+                outgoing.at[r - 1], emb.at[me], ze_s.at[r - 1], ze_r.at[r - 1], {"dp": dp_of(r)}
+            )
+            copy.start()
+            ze.append(copy)
+
+    pm = []
+    for r in range(1, n):
+        zm[r - 1].wait()
+        source = dp_of(n - r)
+        for q in range(1, plane):
+            piece = mblk.at[source, my_rows, my_cols]
+            copy = remote(
+                piece,
+                piece,
+                pm_s.at[r - 1, q - 1],
+                pm_r.at[r - 1, q - 1],
+                at_plane(g, lax.rem(st + q, plane)),
+            )
+            copy.start()
+            pm.append(copy)
+
+    for copy in zc:
+        copy.wait()
+    grads = jnp.zeros((rows, cols), F32)
+    for r in range(n):
+        place = (
+            lax.broadcasted_iota(jnp.int32, (rows, slots), 1) + r * slots == tgt_c
+        ).astype(F32).astype(BF16)
+        block = cot[me] if r == 0 else cot_in[r]
+        grads = grads + jnp.dot(place, block, preferred_element_type=F32)
+    grads = grads * gain
+    values = masked[...]
+    inners = send_stat(1, jnp.sum(grads * values, axis=1, keepdims=True))
+    inner = take_stat(1, inners) / D
+    back = (scale * grads - values * (scale * scale * scale * inner)).astype(BF16)
+    back = (back.astype(F32) * valid).astype(BF16)
+    back_all[me] = back
+
+    brows = rows // BCHUNKS
+
+    def hop(j, c, side):
+        piece = back_all.at[j, pl.ds(c * brows, brows), :]
+        return remote(
+            piece,
+            piece,
+            bk_s.at[side, j, c],
+            bk_r.at[j, c],
+            {"dp": jnp.clip(me + (1 if side == 0 else -1), 0, n - 1)},
+        )
+
+    for c in range(BCHUNKS):
+
+        @pl.when(me < n - 1)
+        def _():
+            hop(me, c, 0).start()
+
+        @pl.when(me > 0)
+        def _():
+            hop(me, c, 1).start()
+
+    gm_copies = []
+    for r in range(1, n):
+        for q in range(1, plane):
+            pm[(r - 1) * (plane - 1) + q - 1].wait()
+        piece = mblk.at[dp_of(n - r), :, my_cols]
+        copy = remote(piece, piece, gm_s.at[r - 1], gm_r.at[r - 1], {"group": 1 - g})
+        copy.start()
+        gm_copies.append(copy)
+
+    def partial(gg, ss):
+        start = pl.multiple_of((gg * plane + ss) * gcols, gcols)
+        return lax.dot_general(
+            back_all[me],
+            w[pl.ds(start, gcols), :],
+            (((1,), (1,)), ((), ())),
+            preferred_element_type=F32,
+        )
+
+    po = []
+    for q in range(plane):
+        slot = (q + 1) % plane
+        pair_out[slot] = partial(1 - g, lax.rem(st + slot, plane)).astype(BF16)
+        copy = remote(
+            pair_out.at[slot], pair_in.at[slot], po_s.at[slot], po_r.at[slot], {"group": 1 - g}
+        )
+        copy.start()
+        po.append(copy)
+    ps = []
+    for q in range(plane):
+        slot = (q + 1) % plane
+        mine = partial(g, lax.rem(st + slot, plane))
+        po[q].wait()
+        mine = mine + pair_in[slot].astype(F32)
+        if slot == 0:
+            gm[...] = mine
+        else:
+            plane_out[slot - 1] = mine.astype(BF16)
+            copy = remote(
+                plane_out.at[slot - 1],
+                plane_in.at[slot - 1],
+                pl_s.at[slot - 1],
+                pl_r.at[slot - 1],
+                at_plane(g, lax.rem(st + slot, plane)),
+            )
+            copy.start()
+            ps.append(copy)
+
+    for t in range(1, n):
+        for c in range(BCHUNKS):
+
+            @pl.when(me - t >= 0)
+            def _():
+                hop(me - t, c, 0).wait_recv()
+
+            @pl.when((me - t >= 0) & (me < n - 1))
+            def _():
+                hop(me - t, c, 0).start()
+
+            @pl.when(me + t <= n - 1)
+            def _():
+                hop(me + t, c, 1).wait_recv()
+
+            @pl.when((me + t <= n - 1) & (me > 0))
+            def _():
+                hop(me + t, c, 1).start()
+
+    for copy in ps:
+        copy.wait()
+    total = gm[...]
+    for q in range(plane - 1):
+        total = total + plane_in[q].astype(F32)
+    gm[...] = total
+    for copy in ze:
+        copy.wait()
+    for copy in gm_copies:
+        copy.wait()
+    for t in range(n):
+        for c in range(BCHUNKS):
+
+            @pl.when((me - t >= 0) & (me < n - 1))
+            def _():
+                hop(me - t, c, 0).wait_send()
+
+            @pl.when((me + t <= n - 1) & (me > 0))
+            def _():
+                hop(me + t, c, 1).wait_send()
+
+
+def weight_kernel(m_ref, b_ref, o_ref):
+    o_ref[...] = lax.dot_general(
+        m_ref[...], b_ref[...], (((0,), (0,)), ((), ())), preferred_element_type=F32
+    )
+
+
+def fast(sizes, merged, counts, owners, w_merge, norm_gain, cotangent):
+    n, groups, sections, tensors = sizes
+    plane = sections * tensors
+    shards = groups * plane
+    rows, deep = merged.shape
+    cols = w_merge.shape[1]
+    slots = cotangent.shape[2]
+    dblock = deep // n
+    gcols = deep // shards
+    wide = -(-rows // 128) * 128
+    vmem = pl.BlockSpec(memory_space=pltpu.VMEM)
+    dma = pltpu.SemaphoreType.DMA
+    emb, gm, mblk, back_all = pl.pallas_call(
+        functools.partial(main_kernel, sizes),
+        name="exchange",
+        out_shape=(
+            jax.ShapeDtypeStruct((n, slots, cols), BF16),
+            jax.ShapeDtypeStruct((rows, gcols), F32),
+            jax.ShapeDtypeStruct((n, rows, dblock), BF16),
+            jax.ShapeDtypeStruct((n, rows, cols), BF16),
+        ),
+        in_specs=[
+            vmem,
+            vmem,
+            pl.BlockSpec(memory_space=pltpu.SMEM),
+            vmem,
+            pl.BlockSpec(memory_space=pl.ANY),
+            vmem,
+            vmem,
+        ],
+        out_specs=(vmem, vmem, vmem, vmem),
+        scratch_shapes=[
+            pltpu.VMEM((deep, cols), BF16),
+            pltpu.VMEM((n, slots, cols), BF16),
+            pltpu.VMEM((n - 1, slots, cols), BF16),
+            pltpu.VMEM((rows, cols), F32),
+            pltpu.VMEM((2, 8, wide), F32),
+            pltpu.VMEM((2, shards, 8, wide), F32),
+            pltpu.VMEM((plane, rows, gcols), BF16),
+            pltpu.VMEM((plane, rows, gcols), BF16),
+            pltpu.VMEM((plane - 1, rows, gcols), BF16),
+            pltpu.VMEM((plane - 1, rows, gcols), BF16),
+            dma((WCHUNKS,)),
+            dma((n - 1,)),
+            dma((n - 1,)),
+            dma((n - 1,)),
+            dma((n - 1,)),
+            dma((n - 1,)),
+            dma((n - 1,)),
+            dma((2, shards - 1)),
+            dma((2, shards - 1)),
+            dma((n - 1, plane - 1)),
+            dma((n - 1, plane - 1)),
+            dma((n - 1,)),
+            dma((n - 1,)),
+            dma((2, n, BCHUNKS)),
+            dma((n, BCHUNKS)),
+            dma((plane,)),
+            dma((plane,)),
+            dma((plane - 1,)),
+            dma((plane - 1,)),
+        ],
+        compiler_params=pltpu.CompilerParams(collective_id=0, has_side_effects=True),
+    )(
+        owners,
+        owners.reshape(1, rows),
+        counts,
+        merged,
+        w_merge,
+        norm_gain.reshape(1, cols),
+        cotangent[0],
+    )
+    tile = 256
+    grad_weight = pl.pallas_call(
+        weight_kernel,
+        name="weight",
+        grid=(dblock // tile,),
+        out_shape=jax.ShapeDtypeStruct((dblock, cols), F32),
+        in_specs=[
+            pl.BlockSpec((n * rows, tile), lambda i: (0, i)),
+            pl.BlockSpec((n * rows, cols), lambda i: (0, 0)),
+        ],
+        out_specs=pl.BlockSpec((tile, cols), lambda i: (i, 0)),
+    )(mblk.reshape(n * rows, dblock), back_all.reshape(n * rows, cols))
+    return emb[None], gm, grad_weight
+
+
 def solution(mesh):
+    sizes = tuple(mesh.shape[name] for name in ("dp", "group", "section", "tensor"))
+
+    def choose(merged, counts, owners, w_merge, norm_gain, cotangent):
+        n, groups, sections, tensors = sizes
+        plane = sections * tensors
+        rows, deep = merged.shape
+        cols = w_merge.shape[1]
+        slots = cotangent.shape[2]
+        fits = (
+            groups == 2
+            and n > 1
+            and plane > 1
+            and rows % (plane * 16) == 0
+            and rows % (BCHUNKS * 16) == 0
+            and deep % (n * groups * 128) == 0
+            and deep % (n * 256) == 0
+            and deep % (groups * plane * 128) == 0
+            and deep % (WCHUNKS * 128) == 0
+            and cols % 128 == 0
+            and slots % 16 == 0
+        )
+        if fits:
+            return fast(sizes, merged, counts, owners, w_merge, norm_gain, cotangent)
+        return on_device(merged, counts, owners, w_merge, norm_gain, cotangent)
+
     placed = (
         P("dp", None),
         P("dp"),
@@ -74,7 +553,7 @@
         P("dp", None, None, ("group", "section", "tensor")),
     )
     return jax.shard_map(
-        on_device,
+        choose,
         mesh=mesh,
         in_specs=placed,
         out_specs=(

time: 183 us -> 85.3 us (0.47)
  blocking collectives: 129 us -> 0 us
  Pallas kernels: 0 us -> 81.3 us
  matrix products: 23.9 us -> 0 us
  between operations: 15.5 us -> 0.66 us
  other arithmetic: 6.04 us -> 0 us
  local copies, waits for them, and re-layouts: 7.84 us -> 3.11 us
    all_to_all x3 -> x0, blocking collectives: 115 us -> none  [the longest x1 64.7 us: on_device(): lax.all_to_all(merged, 'dp', split_axis=1, concat_axis=0, tiled=True)]
    pallas_call x0 -> x2, Pallas kernels: none -> 81.3 us  [the longest x1 74.3 us: fast(): pl.pallas_call(functools.partial(main_kernel, sizes), name='exchange', ou...]
    dot_general x4 -> x0, matrix products: 23.9 us -> none  [the longest x1 9.72 us: on_device(): lax.dot_general(back, w_merge, (((1,), (1,)), ((), ())), preferred_elemen...]
    psum x1 -> x0, blocking collectives: 14.3 us -> none  [on_device(): lax.psum(jnp.sum(values * values, axis=2), ('group', 'section', 'tensor'))]
    unnamed x8 -> x7, local copies, waits for them, and re-layouts: 7.42 us -> 3.11 us
    reduce_sum x3 -> x0, other arithmetic: 1.89 us -> none  [the longest x1 0.74 us: on_device(): count_of = jnp.sum(jnp.where(picked, counts[None, :], 0), axis=1)]
  transfers between devices with their start and end apart: 2 -> 0, of which waited for: 0 -> 0; matrix products, arithmetic and copies ran while one was open for 12% -> 0% of each run, Pallas kernels for 0% -> 0%
where the time goes in v1:
time: 85.3 us; the launch traced here: 85.1 us
  Pallas kernels  81.3 us (95%)
  local copies, waits for them, and re-layouts  3.11 us (4%)
    pallas_call x1, Pallas kernels, fast(): pl.pallas_call(functools.partial(main_kernel, sizes), name='exchange', ou...  74.3 us
    pallas_call x1, Pallas kernels, fast(): pl.pallas_call(weight_kernel, name='weight', grid=(dblock // tile,), out_...  7.03 us
    unnamed x7, local copies, waits for them, and re-layouts  3.11 us

profile of v1, /device:TPU:0, one launch (start us, length us, event | category | flops | bytes accessed | tf_op | source)
XLA Modules:
  0.0 85.1 jit_solution(8231740149522107424)
XLA Ops:
  0.6 1.4 %copy.9.own_col = s32[192,1]{1,0:T(8,128)} copy(s32[192,1]{0,1:T(1,128)} %param.8) | data formatting | bytes 1536 | tf_op args[2]
  2.1 74.3 %exchange.1 = (bf16[4,96,1024]{2,1,0:T(8,128)(2,1)}, f32[192,640]{1,0:T(8,128)}, bf16[4,192,1280]{2,1,0:T(8,128)(2,1)}, bf16[4,192,1024]{2,1,0:T(8,128)(2,1)}) custom-call(s32[192,1]{1,0:T(8,128)} %copy.9.own_col, s32[1,192]{1,0:T(1,128)} %bitcast.11, s32[2]{0:T(128)} %counts.1, bf16[192,5120]{1,0:T(8,128)(2,1)} %merged.1, bf16[5120,1024]{1,0:T(8,128)(2,1)} %w_hbm.1, ...), custom_call_target="tpu_custom_call" | custom-call | tf_op jit(solution)/shard_map/exchange/pallas_call | solution.py:446
  76.4 0.0 copy-start
  76.4 0.0 copy-start.1
  76.4 7.0 %weight.1 = f32[1280,1024]{1,0:T(8,128)} custom-call(bf16[768,1280]{1,0:T(8,128)(2,1)} %bitcast.6, bf16[768,1024]{1,0:T(8,128)(2,1)} %bitcast.7), custom_call_target="tpu_custom_call" | custom-call | tf_op jit(solution)/shard_map/weight/pallas_call | solution.py:507
  83.4 0.0 copy-done
  83.4 0.9 %copy.12 = bf16[1,4,96,1024]{3,2,1,0:T(8,128)(2,1)} copy(bf16[1,4,96,1024]{3,2,1,0:T(8,128)(2,1)S(1)} %bitcast.9) | data formatting | bytes 1572864
  84.3 0.0 copy-done.1
  84.3 0.8 copy.13
Async XLA Ops:
  76.4 7.1 %copy-start = (bf16[4,96,1024]{2,1,0:T(8,128)(2,1)S(1)}, bf16[4,96,1024]{2,1,0:T(8,128)(2,1)}, u32[]{:S(2)}) copy-start(bf16[4,96,1024]{2,1,0:T(8,128)(2,1)} %get-tuple-element.7) | copy-start | bytes 2359300
  76.4 7.9 %copy-start.1 = (f32[192,640]{1,0:T(8,128)S(1)}, f32[192,640]{1,0:T(8,128)}, u32[]{:S(2)}) copy-start(f32[192,640]{1,0:T(8,128)} %get-tuple-element.15) | copy-start | bytes 1474564

commit v2 on v1

--- a/solution.py
+++ b/solution.py
@@ -12,7 +12,7 @@
 F32 = jnp.float32
 BF16 = jnp.bfloat16
 WCHUNKS = 5
-BCHUNKS = 4
+BCHUNKS = 2
 
 
 def on_device(merged, counts, owners, w_merge, norm_gain, cotangent):
@@ -86,20 +86,21 @@
 
 def main_kernel(
     sizes,
-    own_col,
     own_row,
     counts,
     merged,
     w_hbm,
     gain_ref,
-    cot,
+    cot_hbm,
     emb,
     gm,
     mblk,
     back_all,
     w,
-    cot_in,
-    outgoing,
+    cots,
+    mix,
+    mix_out,
+    info,
     masked,
     stat_out,
     stat_in,
@@ -108,20 +109,21 @@
     plane_out,
     plane_in,
     w_sem,
+    cot_sem,
     zm_s,
     zm_r,
-    zc_s,
-    zc_r,
-    ze_s,
-    ze_r,
+    ck_s,
+    ck_r,
+    in_s,
+    in_r,
     st_s,
     st_r,
     pm_s,
     pm_r,
     gm_s,
     gm_r,
-    bk_s,
-    bk_r,
+    mx_s,
+    mx_r,
     po_s,
     po_r,
     pl_s,
@@ -132,7 +134,7 @@
     shards = groups * plane
     rows, deep = merged.shape
     cols = w.shape[1]
-    slots = cot.shape[1]
+    slots = cots.shape[2]
     dblock = deep // n
     half = dblock // groups
     part = rows // plane
@@ -161,6 +163,8 @@
             device_id=at_plane(other // plane, lax.rem(other, plane)),
             device_id_type=MESH,
         )
+    cot_load = pltpu.make_async_copy(cot_hbm, cots.at[me], cot_sem)
+    cot_load.start()
     wrows = deep // WCHUNKS
     wcopies = []
     for c in range(WCHUNKS):
@@ -173,8 +177,26 @@
 
     my_rows = pl.ds(pl.multiple_of(st * part, part), part)
     my_cols = pl.ds(pl.multiple_of(g * half, half), half)
+    def step_to(side):
+        return {"dp": jnp.clip(me + (1 if side == 0 else -1), 0, n - 1)}
+
+    def cot_hop(p, b, side):
+        piece = cots.at[p, b]
+        return remote(piece, piece, ck_s.at[p, b], ck_r.at[p, b], step_to(side))
+
+    cot_load.wait()
+    for k in range(n - 1):
+        b = n - 1 - k
+
+        @pl.when(me < b)
+        def _():
+            cot_hop(me, b, 0).start()
+
+        @pl.when(me > k)
+        def _():
+            cot_hop(me, k, 1).start()
+
     zm = []
-    zc = []
     for r in range(1, n):
         to = dp_of(r)
         copy = remote(
@@ -186,11 +208,6 @@
         )
         copy.start()
         zm.append(copy)
-    for r in range(1, n):
-        to = dp_of(r)
-        copy = remote(cot.at[to], cot_in.at[n - r], zc_s.at[r - 1], zc_r.at[n - r - 1], {"dp": to})
-        copy.start()
-        zc.append(copy)
 
     acc = jnp.zeros((rows, cols), F32)
     for c in range(WCHUNKS):
@@ -244,43 +261,67 @@
 
     squares = send_stat(0, jnp.sum(values * values, axis=1, keepdims=True))
 
-    oc = own_col[...]
     orow = own_row[...]
-    hits_c = (oc == lax.broadcasted_iota(jnp.int32, (rows, n), 1)).astype(F32)
-    hits_r = (orow == lax.broadcasted_iota(jnp.int32, (n, rows), 0)).astype(F32)
+    hits = (orow == lax.broadcasted_iota(jnp.int32, (n, rows), 0)).astype(F32)
     i0 = lax.broadcasted_iota(jnp.int32, (rows, rows), 0)
     i1 = lax.broadcasted_iota(jnp.int32, (rows, rows), 1)
-    lower = (i1 < i0).astype(F32).astype(BF16)
     upper = (i0 < i1).astype(F32).astype(BF16)
-    before_c = jnp.dot(lower, hits_c.astype(BF16), preferred_element_type=F32)
-    before_r = jnp.dot(hits_r.astype(BF16), upper, preferred_element_type=F32)
-    slot_c = jnp.sum(before_c * hits_c, axis=1, keepdims=True).astype(jnp.int32)
-    slot_r = jnp.sum(before_r * hits_r, axis=0, keepdims=True).astype(jnp.int32)
-    rel_c = jnp.where(oc < me, oc - me + n, oc - me)
-    rel_r = jnp.where(orow < me, orow - me + n, orow - me)
-    tgt_c = rel_c * slots + slot_c
-    tgt_r = rel_r * slots + slot_r
+    before = jnp.dot(hits.astype(BF16), upper, preferred_element_type=F32)
+    slot_row = jnp.sum(before * hits, axis=0, keepdims=True)
+    tgt_row = orow * slots + slot_row.astype(jnp.int32)
+    same = i0 == i1
+    tgt_col = jnp.sum(jnp.where(same, tgt_row, 0), axis=1, keepdims=True)
     gain = gain_ref[...]
 
+    def gather_place(p, target):
+        ids = lax.broadcasted_iota(jnp.int32, (target.shape[0], slots), 1) + p * slots
+        return (ids == target).astype(F32).astype(BF16)
+
+    def scatter_place(target):
+        ids = lax.broadcasted_iota(jnp.int32, (slots, rows), 0) + me * slots
+        return (ids == target).astype(F32).astype(BF16)
+
     mblk[me] = merged[:, pl.ds(pl.multiple_of(me * dblock, dblock), dblock)]
 
     scale = lax.rsqrt(take_stat(0, squares) / D + 1e-05)
-    normed = (values * scale * gain).astype(BF16)
-    ze = []
-    for r in range(n):
-        place = (
-            lax.broadcasted_iota(jnp.int32, (slots, rows), 0) + r * slots == tgt_r
-        ).astype(F32).astype(BF16)
-        block = jnp.dot(place, normed, preferred_element_type=F32).astype(BF16)
-        if r == 0:
-            emb[me] = block
-        else:
-            outgoing[r - 1] = block
-            copy = remote(
-                outgoing.at[r - 1], emb.at[me], ze_s.at[r - 1], ze_r.at[r - 1], {"dp": dp_of(r)}
-            )
-            copy.start()
-            ze.append(copy)
+    emb[me] = jnp.dot(
+        scatter_place(tgt_row),
+        (values * scale * gain).astype(BF16),
+        preferred_element_type=F32,
+    ).astype(BF16)
+
+    for t in range(1, n):
+        for k in range(n):
+            b = n - 1 - k
+
+            @pl.when((me >= t) & (me < b))
+            def _():
+                cot_hop(me - t, b, 0).wait_recv()
+                cot_hop(me - t, b, 0).start()
+
+            @pl.when((me + t <= n - 1) & (me > k))
+            def _():
+                cot_hop(me + t, k, 1).wait_recv()
+                cot_hop(me + t, k, 1).start()
+
+    for t in range(1, n):
+
+        @pl.when(me >= t)
+        def _():
+            cot_hop(me - t, me, 0).wait_recv()
+
+        @pl.when(me + t <= n - 1)
+        def _():
+            cot_hop(me + t, me, 1).wait_recv()
+
+    grads = jnp.zeros((rows, cols), F32)
+    for p in range(n):
+        grads = grads + jnp.dot(
+            gather_place(p, tgt_col), cots[p, me], preferred_element_type=F32
+        )
+    grads = grads * gain
+    values = masked[...]
+    inners = send_stat(1, jnp.sum(grads * values, axis=1, keepdims=True))
 
     pm = []
     for r in range(1, n):
@@ -298,44 +339,103 @@
             copy.start()
             pm.append(copy)
 
-    for copy in zc:
-        copy.wait()
-    grads = jnp.zeros((rows, cols), F32)
-    for r in range(n):
-        place = (
-            lax.broadcasted_iota(jnp.int32, (rows, slots), 1) + r * slots == tgt_c
-        ).astype(F32).astype(BF16)
-        block = cot[me] if r == 0 else cot_in[r]
-        grads = grads + jnp.dot(place, block, preferred_element_type=F32)
-    grads = grads * gain
-    values = masked[...]
-    inners = send_stat(1, jnp.sum(grads * values, axis=1, keepdims=True))
     inner = take_stat(1, inners) / D
-    back = (scale * grads - values * (scale * scale * scale * inner)).astype(BF16)
-    back = (back.astype(F32) * valid).astype(BF16)
+    near = valid * scale
+    far = valid * (scale * scale * scale * inner)
+    back = (near * grads - values * far).astype(BF16)
     back_all[me] = back
 
+    def as_line(column):
+        return jnp.sum(jnp.where(eye, column, 0.0), axis=0, keepdims=True)
+
+    info[me, 0:1] = as_line(tgt_col.astype(F32))
+    info[me, 1:2] = as_line(scale)
+    info[me, 2:3] = as_line(near)
+    info[me, 3:4] = as_line(far)
+    info[me, 4:8] = jnp.zeros((4, wide), F32)
+    infos = []
+    for r in range(1, n):
+        copy = remote(
+            info.at[me], info.at[me], in_s.at[r - 1], in_r.at[r - 1], {"dp": dp_of(r)}
+        )
+        copy.start()
+        infos.append(copy)
+
     brows = rows // BCHUNKS
 
-    def hop(j, c, side):
-        piece = back_all.at[j, pl.ds(c * brows, brows), :]
+    def mix_hop(slot, b, c, side):
+        piece = pl.ds(c * brows, brows)
         return remote(
-            piece,
-            piece,
-            bk_s.at[side, j, c],
-            bk_r.at[j, c],
-            {"dp": jnp.clip(me + (1 if side == 0 else -1), 0, n - 1)},
-        )
-
+            mix_out.at[slot, piece, :],
+            mix.at[b, piece, :],
+            mx_s.at[slot, c],
+            mx_r.at[b, c],
+            step_to(side),
+        )
+
+    packed = values.astype(BF16)
+    mix_out[n] = jnp.where(tgt_col >= (me + 1) * slots, packed, back)
+    mix_out[me] = jnp.where(tgt_col < me * slots, packed, back)
     for c in range(BCHUNKS):
 
         @pl.when(me < n - 1)
         def _():
-            hop(me, c, 0).start()
+            mix_hop(n, me, c, 0).start()
 
         @pl.when(me > 0)
         def _():
-            hop(me, c, 1).start()
+            mix_hop(me, me, c, 1).start()
+
+    def take_block(b, side):
+        def column(line):
+            return jnp.sum(jnp.where(eye, info[b, line : line + 1], 0.0), axis=1, keepdims=True)
+
+        target = column(0).astype(jnp.int32)
+        r_scale, r_near, r_far = column(1), column(2), column(3)
+        first, last = (me, n) if side == 0 else (0, me + 1)
+        for c in range(BCHUNKS):
+            lo, hi = c * brows, (c + 1) * brows
+            aim = target[lo:hi]
+
+            def add(p, total):
+                return total + jnp.dot(
+                    gather_place(p, aim), cots[p, b], preferred_element_type=F32
+                )
+
+            want = lax.fori_loop(first, last, add, jnp.zeros((brows, cols), F32)) * gain
+            mix_hop(b, b, c, side).wait_recv()
+            got = mix[b, lo:hi, :]
+            whole = (r_near[lo:hi] * want - got.astype(F32) * r_far[lo:hi]).astype(BF16)
+            if side == 0:
+                whole = jnp.where(aim >= me * slots, whole, got)
+                onward = jnp.where(aim >= (me + 1) * slots, got, whole)
+                more = me < n - 1
+            else:
+                whole = jnp.where(aim < (me + 1) * slots, whole, got)
+                onward = jnp.where(aim < me * slots, got, whole)
+                more = me > 0
+            back_all[b, lo:hi, :] = whole
+            mix_out[b, lo:hi, :] = onward
+
+            @pl.when(more)
+            def _():
+                mix_hop(b, b, c, side).start()
+
+        line = info[b, 0:1, 0:rows].astype(jnp.int32)
+        emb[b] = jnp.dot(
+            scatter_place(line),
+            (mix[b].astype(F32) * r_scale * gain).astype(BF16),
+            preferred_element_type=F32,
+        ).astype(BF16)
+
+    def take_blocks(t):
+        @pl.when(me >= t)
+        def _():
+            take_block(me - t, 0)
+
+        @pl.when(me + t <= n - 1)
+        def _():
+            take_block(me + t, 1)
 
     gm_copies = []
     for r in range(1, n):
@@ -364,6 +464,9 @@
         )
         copy.start()
         po.append(copy)
+    for copy in infos:
+        copy.wait()
+    take_blocks(1)
     ps = []
     for q in range(plane):
         slot = (q + 1) % plane
@@ -384,24 +487,8 @@
             copy.start()
             ps.append(copy)
 
-    for t in range(1, n):
-        for c in range(BCHUNKS):
-
-            @pl.when(me - t >= 0)
-            def _():
-                hop(me - t, c, 0).wait_recv()
-
-            @pl.when((me - t >= 0) & (me < n - 1))
-            def _():
-                hop(me - t, c, 0).start()
-
-            @pl.when(me + t <= n - 1)
-            def _():
-                hop(me + t, c, 1).wait_recv()
-
-            @pl.when((me + t <= n - 1) & (me > 0))
-            def _():
-                hop(me + t, c, 1).start()
+    for t in range(2, n):
+        take_blocks(t)
 
     for copy in ps:
         copy.wait()
@@ -409,20 +496,29 @@
     for q in range(plane - 1):
         total = total + plane_in[q].astype(F32)
     gm[...] = total
-    for copy in ze:
-        copy.wait()
     for copy in gm_copies:
         copy.wait()
     for t in range(n):
+        for k in range(n):
+            b = n - 1 - k
+
+            @pl.when((me >= t) & (me < b))
+            def _():
+                cot_hop(me - t, b, 0).wait_send()
+
+            @pl.when((me + t <= n - 1) & (me > k))
+            def _():
+                cot_hop(me + t, k, 1).wait_send()
+
         for c in range(BCHUNKS):
 
-            @pl.when((me - t >= 0) & (me < n - 1))
+            @pl.when((me >= t) & (me < n - 1))
             def _():
-                hop(me - t, c, 0).wait_send()
+                mix_hop(n if t == 0 else me - t, me - t, c, 0).wait_send()
 
             @pl.when((me + t <= n - 1) & (me > 0))
             def _():
-                hop(me + t, c, 1).wait_send()
+                mix_hop(me + t, me + t, c, 1).wait_send()
 
 
 def weight_kernel(m_ref, b_ref, o_ref):
@@ -454,18 +550,19 @@
         ),
         in_specs=[
             vmem,
-            vmem,
             pl.BlockSpec(memory_space=pltpu.SMEM),
             vmem,
             pl.BlockSpec(memory_space=pl.ANY),
             vmem,
-            vmem,
+            pl.BlockSpec(memory_space=pl.ANY),
         ],
         out_specs=(vmem, vmem, vmem, vmem),
         scratch_shapes=[
             pltpu.VMEM((deep, cols), BF16),
-            pltpu.VMEM((n, slots, cols), BF16),
-            pltpu.VMEM((n - 1, slots, cols), BF16),
+            pltpu.VMEM((n, n, slots, cols), BF16),
+            pltpu.VMEM((n, rows, cols), BF16),
+            pltpu.VMEM((n + 1, rows, cols), BF16),
+            pltpu.VMEM((n, 8, wide), F32),
             pltpu.VMEM((rows, cols), F32),
             pltpu.VMEM((2, 8, wide), F32),
             pltpu.VMEM((2, shards, 8, wide), F32),
@@ -474,10 +571,11 @@
             pltpu.VMEM((plane - 1, rows, gcols), BF16),
             pltpu.VMEM((plane - 1, rows, gcols), BF16),
             dma((WCHUNKS,)),
+            dma,
             dma((n - 1,)),
             dma((n - 1,)),
-            dma((n - 1,)),
-            dma((n - 1,)),
+            dma((n, n)),
+            dma((n, n)),
             dma((n - 1,)),
             dma((n - 1,)),
             dma((2, shards - 1)),
@@ -486,7 +584,7 @@
             dma((n - 1, plane - 1)),
             dma((n - 1,)),
             dma((n - 1,)),
-            dma((2, n, BCHUNKS)),
+            dma((n + 1, BCHUNKS)),
             dma((n, BCHUNKS)),
             dma((plane,)),
             dma((plane,)),
@@ -495,7 +593,6 @@
         ],
         compiler_params=pltpu.CompilerParams(collective_id=0, has_side_effects=True),
     )(
-        owners,
         owners.reshape(1, rows),
         counts,
         merged,

time: 85.3 us -> 81.4 us (0.954)
  Pallas kernels: 81.3 us -> 78.8 us
  local copies, waits for them, and re-layouts: 3.11 us -> 1.67 us
    pallas_call x1, Pallas kernels: 74.3 us -> 71.8 us  [fast(): pl.pallas_call(functools.partial(main_kernel, sizes), name='exchange', ou...]
    unnamed x7 -> x6, local copies, waits for them, and re-layouts: 3.11 us -> 1.67 us
where the time goes in v2:
time: 81.4 us; the launch traced here: 81.2 us
  Pallas kernels  78.8 us (97%)
  local copies, waits for them, and re-layouts  1.67 us (2%)
    pallas_call x1, Pallas kernels, fast(): pl.pallas_call(functools.partial(main_kernel, sizes), name='exchange', ou...  71.8 us
    pallas_call x1, Pallas kernels, fast(): pl.pallas_call(weight_kernel, name='weight', grid=(dblock // tile,), out_...  7.03 us
    unnamed x6, local copies, waits for them, and re-layouts  1.67 us

profile of v2, /device:TPU:0, one launch (start us, length us, event | category | flops | bytes accessed | tf_op | source)
XLA Modules:
  0.0 81.2 jit_solution(14677492635025489975)
XLA Ops:
  0.6 71.8 %exchange.1 = (bf16[4,96,1024]{2,1,0:T(8,128)(2,1)}, f32[192,640]{1,0:T(8,128)}, bf16[4,192,1280]{2,1,0:T(8,128)(2,1)}, bf16[4,192,1024]{2,1,0:T(8,128)(2,1)}) custom-call(s32[1,192]{1,0:T(1,128)} %bitcast.11, s32[2]{0:T(128)} %counts.1, bf16[192,5120]{1,0:T(8,128)(2,1)} %merged.1, bf16[5120,1024]{1,0:T(8,128)(2,1)} %w_hbm.1, f32[1,1024]{1,0:T(1,128)} %bitcast.10, ...), custom_call_target="tpu_custom_call" | custom-call | tf_op jit(solution)/shard_map/exchange/pallas_call | solution.py:542
  72.5 0.0 copy-start
  72.5 0.0 copy-start.1
  72.5 7.0 %weight.1 = f32[1280,1024]{1,0:T(8,128)} custom-call(bf16[768,1280]{1,0:T(8,128)(2,1)} %bitcast.6, bf16[768,1024]{1,0:T(8,128)(2,1)} %bitcast.7), custom_call_target="tpu_custom_call" | custom-call | tf_op jit(solution)/shard_map/weight/pallas_call | solution.py:604
  79.5 0.0 copy-done
  79.5 0.9 %copy.11 = bf16[1,4,96,1024]{3,2,1,0:T(8,128)(2,1)} copy(bf16[1,4,96,1024]{3,2,1,0:T(8,128)(2,1)S(1)} %bitcast.9) | data formatting | bytes 1572864
  80.4 0.0 copy-done.1
  80.4 0.8 copy.12
Async XLA Ops:
  72.5 7.1 %copy-start = (bf16[4,96,1024]{2,1,0:T(8,128)(2,1)S(1)}, bf16[4,96,1024]{2,1,0:T(8,128)(2,1)}, u32[]{:S(2)}) copy-start(bf16[4,96,1024]{2,1,0:T(8,128)(2,1)} %get-tuple-element.7) | copy-start | bytes 2359300
  72.5 7.9 %copy-start.1 = (f32[192,640]{1,0:T(8,128)S(1)}, f32[192,640]{1,0:T(8,128)}, u32[]{:S(2)}) copy-start(f32[192,640]{1,0:T(8,128)} %get-tuple-element.15) | copy-start | bytes 1474564

commit v3 on v2

--- a/solution.py
+++ b/solution.py
@@ -13,6 +13,7 @@
 BF16 = jnp.bfloat16
 WCHUNKS = 5
 BCHUNKS = 2
+TILE = 256
 
 
 def on_device(merged, counts, owners, w_merge, norm_gain, cotangent):
@@ -180,34 +181,20 @@
     def step_to(side):
         return {"dp": jnp.clip(me + (1 if side == 0 else -1), 0, n - 1)}
 
-    def cot_hop(p, b, side):
+    def cot_hop(p, b, side, own=False):
         piece = cots.at[p, b]
-        return remote(piece, piece, ck_s.at[p, b], ck_r.at[p, b], step_to(side))
-
-    cot_load.wait()
+        return remote(cot_hbm.at[b] if own else piece, piece, ck_s.at[p, b], ck_r.at[p, b], step_to(side))
+
     for k in range(n - 1):
         b = n - 1 - k
 
         @pl.when(me < b)
         def _():
-            cot_hop(me, b, 0).start()
+            cot_hop(me, b, 0, True).start()
 
         @pl.when(me > k)
         def _():
-            cot_hop(me, k, 1).start()
-
-    zm = []
-    for r in range(1, n):
-        to = dp_of(r)
-        copy = remote(
-            merged.at[my_rows, pl.ds(pl.multiple_of(to * dblock + g * half, half), half)],
-            mblk.at[me, my_rows, my_cols],
-            zm_s.at[r - 1],
-            zm_r.at[r - 1],
-            {"dp": to},
-        )
-        copy.start()
-        zm.append(copy)
+            cot_hop(me, k, 1, True).start()
 
     acc = jnp.zeros((rows, cols), F32)
     for c in range(WCHUNKS):
@@ -304,6 +291,19 @@
                 cot_hop(me + t, k, 1).wait_recv()
                 cot_hop(me + t, k, 1).start()
 
+    zm = []
+    for r in range(1, n):
+        to = dp_of(r)
+        copy = remote(
+            merged.at[my_rows, pl.ds(pl.multiple_of(to * dblock + g * half, half), half)],
+            mblk.at[me, my_rows, my_cols],
+            zm_s.at[r - 1],
+            zm_r.at[r - 1],
+            {"dp": to},
+        )
+        copy.start()
+        zm.append(copy)
+
     for t in range(1, n):
 
         @pl.when(me >= t)
@@ -314,6 +314,7 @@
         def _():
             cot_hop(me + t, me, 1).wait_recv()
 
+    cot_load.wait()
     grads = jnp.zeros((rows, cols), F32)
     for p in range(n):
         grads = grads + jnp.dot(
@@ -386,41 +387,44 @@
         def _():
             mix_hop(me, me, c, 1).start()
 
-    def take_block(b, side):
+    def take_chunk(b, side, c):
+        lo, hi = c * brows, (c + 1) * brows
+
         def column(line):
-            return jnp.sum(jnp.where(eye, info[b, line : line + 1], 0.0), axis=1, keepdims=True)
-
-        target = column(0).astype(jnp.int32)
-        r_scale, r_near, r_far = column(1), column(2), column(3)
+            picked = jnp.where(eye[lo:hi], info[b, line : line + 1], 0.0)
+            return jnp.sum(picked, axis=1, keepdims=True)
+
+        aim = column(0).astype(jnp.int32)
+        r_near, r_far = column(2), column(3)
         first, last = (me, n) if side == 0 else (0, me + 1)
-        for c in range(BCHUNKS):
-            lo, hi = c * brows, (c + 1) * brows
-            aim = target[lo:hi]
-
-            def add(p, total):
-                return total + jnp.dot(
-                    gather_place(p, aim), cots[p, b], preferred_element_type=F32
-                )
-
-            want = lax.fori_loop(first, last, add, jnp.zeros((brows, cols), F32)) * gain
-            mix_hop(b, b, c, side).wait_recv()
-            got = mix[b, lo:hi, :]
-            whole = (r_near[lo:hi] * want - got.astype(F32) * r_far[lo:hi]).astype(BF16)
-            if side == 0:
-                whole = jnp.where(aim >= me * slots, whole, got)
-                onward = jnp.where(aim >= (me + 1) * slots, got, whole)
-                more = me < n - 1
-            else:
-                whole = jnp.where(aim < (me + 1) * slots, whole, got)
-                onward = jnp.where(aim < me * slots, got, whole)
-                more = me > 0
-            back_all[b, lo:hi, :] = whole
-            mix_out[b, lo:hi, :] = onward
-
-            @pl.when(more)
-            def _():
-                mix_hop(b, b, c, side).start()
-
+
+        def add(p, total):
+            return total + jnp.dot(
+                gather_place(p, aim), cots[p, b], preferred_element_type=F32
+            )
+
+        want = lax.fori_loop(first, last, add, jnp.zeros((brows, cols), F32)) * gain * r_near
+        mix_hop(b, b, c, side).wait_recv()
+        got = mix[b, lo:hi, :]
+        whole = (want - got.astype(F32) * r_far).astype(BF16)
+        if side == 0:
+            whole = jnp.where(aim >= me * slots, whole, got)
+            onward = jnp.where(aim >= (me + 1) * slots, got, whole)
+            more = me < n - 1
+        else:
+            whole = jnp.where(aim < (me + 1) * slots, whole, got)
+            onward = jnp.where(aim < me * slots, got, whole)
+            more = me > 0
+        mix_out[b, lo:hi, :] = onward
+
+        @pl.when(more)
+        def _():
+            mix_hop(b, b, c, side).start()
+
+        back_all[b, lo:hi, :] = whole
+
+    def embed(b):
+        r_scale = jnp.sum(jnp.where(eye, info[b, 1:2], 0.0), axis=1, keepdims=True)
         line = info[b, 0:1, 0:rows].astype(jnp.int32)
         emb[b] = jnp.dot(
             scatter_place(line),
@@ -429,13 +433,23 @@
         ).astype(BF16)
 
     def take_blocks(t):
+        for c in range(BCHUNKS):
+
+            @pl.when(me >= t)
+            def _():
+                take_chunk(me - t, 0, c)
+
+            @pl.when(me + t <= n - 1)
+            def _():
+                take_chunk(me + t, 1, c)
+
         @pl.when(me >= t)
         def _():
-            take_block(me - t, 0)
+            embed(me - t)
 
         @pl.when(me + t <= n - 1)
         def _():
-            take_block(me + t, 1)
+            embed(me + t)
 
     gm_copies = []
     for r in range(1, n):
@@ -521,10 +535,12 @@
                 mix_hop(me + t, me + t, c, 1).wait_send()
 
 
-def weight_kernel(m_ref, b_ref, o_ref):
+def weight_kernel(m_ref, b_ref, e_ref, g_ref, o_ref, eo_ref, go_ref):
     o_ref[...] = lax.dot_general(
         m_ref[...], b_ref[...], (((0,), (0,)), ((), ())), preferred_element_type=F32
     )
+    eo_ref[...] = e_ref[...]
+    go_ref[...] = g_ref[...]
 
 
 def fast(sizes, merged, counts, owners, w_merge, norm_gain, cotangent):
@@ -600,19 +616,43 @@
         norm_gain.reshape(1, cols),
         cotangent[0],
     )
-    tile = 256
-    grad_weight = pl.pallas_call(
+    tile = TILE
+    steps = dblock // tile
+    pieces = 1
+    while pieces * 2 <= steps and (rows // (pieces * 2)) % 8 == 0:
+        pieces *= 2
+    egot, ggot = n * slots // pieces, rows // pieces
+
+    def piece_map(i):
+        return (jnp.minimum(i, pieces - 1), 0)
+
+    grad_weight, emb, gm = pl.pallas_call(
         weight_kernel,
         name="weight",
-        grid=(dblock // tile,),
-        out_shape=jax.ShapeDtypeStruct((dblock, cols), F32),
+        grid=(steps,),
+        out_shape=(
+            jax.ShapeDtypeStruct((dblock, cols), F32),
+            jax.ShapeDtypeStruct((n * slots, cols), BF16),
+            jax.ShapeDtypeStruct((rows, gcols), F32),
+        ),
         in_specs=[
             pl.BlockSpec((n * rows, tile), lambda i: (0, i)),
             pl.BlockSpec((n * rows, cols), lambda i: (0, 0)),
+            pl.BlockSpec((egot, cols), piece_map),
+            pl.BlockSpec((ggot, gcols), piece_map),
         ],
-        out_specs=pl.BlockSpec((tile, cols), lambda i: (i, 0)),
-    )(mblk.reshape(n * rows, dblock), back_all.reshape(n * rows, cols))
-    return emb[None], gm, grad_weight
+        out_specs=(
+            pl.BlockSpec((tile, cols), lambda i: (i, 0)),
+            pl.BlockSpec((egot, cols), piece_map),
+            pl.BlockSpec((ggot, gcols), piece_map),
+        ),
+    )(
+        mblk.reshape(n * rows, dblock),
+        back_all.reshape(n * rows, cols),
+        emb.reshape(n * slots, cols),
+        gm,
+    )
+    return emb.reshape(1, n, slots, cols), gm, grad_weight
 
 
 def solution(mesh):
@@ -631,11 +671,12 @@
             and rows % (plane * 16) == 0
             and rows % (BCHUNKS * 16) == 0
             and deep % (n * groups * 128) == 0
-            and deep % (n * 256) == 0
+            and deep % (n * TILE) == 0
             and deep % (groups * plane * 128) == 0
             and deep % (WCHUNKS * 128) == 0
             and cols % 128 == 0
             and slots % 16 == 0
+            and (n * slots) % rows == 0
         )
         if fits:
             return fast(sizes, merged, counts, owners, w_merge, norm_gain, cotangent)

time: 81.4 us -> 73.2 us (0.90)
  Pallas kernels: 78.8 us -> 72.3 us
  local copies, waits for them, and re-layouts: 1.67 us -> 0 us
    pallas_call x1, Pallas kernels: 71.8 us -> 64.6 us  [fast(): pl.pallas_call(functools.partial(main_kernel, sizes), name='exchange', ou...]
    unnamed x6 -> x0, local copies, waits for them, and re-layouts: 1.67 us -> none
where the time goes in v3:
time: 73.2 us; the launch traced here: 73 us
  Pallas kernels  72.3 us (99%)
    pallas_call x1, Pallas kernels, fast(): pl.pallas_call(functools.partial(main_kernel, sizes), name='exchange', ou...  64.6 us
    pallas_call x1, Pallas kernels, fast(): pl.pallas_call(weight_kernel, name='weight', grid=(steps,), out_shape=(ja...  7.7 us

profile of v3, /device:TPU:0, one launch (start us, length us, event | category | flops | bytes accessed | tf_op | source)
XLA Modules:
  0.0 73.0 jit_solution(6279217465720138970)
XLA Ops:
  0.6 64.6 %exchange.1 = (bf16[4,96,1024]{2,1,0:T(8,128)(2,1)}, f32[192,640]{1,0:T(8,128)}, bf16[4,192,1280]{2,1,0:T(8,128)(2,1)}, bf16[4,192,1024]{2,1,0:T(8,128)(2,1)}) custom-call(s32[1,192]{1,0:T(1,128)} %bitcast.12, s32[2]{0:T(128)} %counts.1, bf16[192,5120]{1,0:T(8,128)(2,1)} %merged.1, bf16[5120,1024]{1,0:T(8,128)(2,1)} %w_hbm.1, f32[1,1024]{1,0:T(1,128)} %bitcast.11, ...), custom_call_target="tpu_custom_call" | custom-call | tf_op jit(solution)/shard_map/exchange/pallas_call | solution.py:558
  65.3 7.7 %weight.1 = (f32[1280,1024]{1,0:T(8,128)}, bf16[384,1024]{1,0:T(8,128)(2,1)}, f32[192,640]{1,0:T(8,128)}) custom-call(bf16[768,1280]{1,0:T(8,128)(2,1)} %bitcast.7, bf16[768,1024]{1,0:T(8,128)(2,1)} %bitcast.8, bf16[384,1024]{1,0:T(8,128)(2,1)} %bitcast.10, f32[192,640]{1,0:T(8,128)} %get-tuple-element.13.g_ref), custom_call_target="tpu_custom_call" | custom-call | tf_op jit(solution)/shard_map/weight/pallas_call | solution.py:629
